TPU v7x, 128 devices: a whole 4x4x4 slice. The times are simulated.
128 devices in a mesh: comp: 2 (over core), gx: 8 (over x_hi, z), gy: 8 (over x_lo, y).
Axes of the slice: x: 4 (x_hi: 2, x_lo: 2; x = x_hi * 2 + x_lo), y: 4, z: 4, core: 2. Of those that a mesh axis runs over, the one named last changes fastest.
Arguments:
- atmos_state: float32 [10, 20, 256, 1024], P(None, None, ('comp', 'gx'), 'gy'), may hold values from -6 to 6
- atmos_diffusion: float32 [10], replicated, may hold values from 0.03 to 0.12
- remap_atmos: float32 [2048, 128, 128], P(('comp', 'gx', 'gy')), may hold values from -0.1237436867076458 to 1.5237436867076457
- exchange_owner: int32 [2048, 1], P(('comp', 'gx', 'gy')), may hold values from 0 to 63; in each aligned block of 16 rows (0 to 15, 16 to 31, ...) at most 2 rows name the same one
- exchange_slot: int32 [2048], P(('comp', 'gx', 'gy')), may hold values from 0 to 15
- remap_ocean: float32 [2048, 128, 128], P(('comp', 'gx', 'gy')), may hold values from -0.1237436867076458 to 1.5237436867076457
- ocean_owner: int32 [2048, 1], P(('comp', 'gx', 'gy')), may hold values from 0 to 63; in each aligned block of 16 rows (0 to 15, 16 to 31, ...) at most 2 rows name the same one
- ocean_slot: int32 [2048], P(('comp', 'gx', 'gy')), may hold values from 0 to 63
- ocean_state: float32 [4, 8, 512, 1024], P(None, None, 'gx', 'gy'), may hold values from -6 to 6
- ocean_mixing: float32 [4], replicated, may hold values from 0.03 to 0.12
- wet_mask: int32 [512, 1024], P('gx', 'gy'), may hold values 0 or 1
Outputs:
- atmos_next: float32 [10, 20, 256, 1024], P(None, None, ('comp', 'gx'), 'gy')
- ocean_next: float32 [4, 8, 512, 1024], P(None, None, 'gx', 'gy')
- ocean_surface: float32 [4, 256, 1024], P(None, ('comp', 'gx'), 'gy')
Inputs may be any that keep to these rules, and one draw needn't show every extreme that they name: `exchange_owner`: among the rows of one device, no owner appears more than 2 times, and one appears exactly 2 times. `ocean_owner`: among the rows of one device, no owner appears more than 2 times, and one appears exactly 2 times.
All inputs are finite; a program needn't handle non-finite values. No bound on the sum of `wet_mask` on one device may be relied on, other than what follows from the above.
Results may differ from a plain program's by a relative error of at most 0.000088.
Values sent between devices are 32-bit elements; how exact they have to be, the bound alone decides.
A program may use at most 128 MiB of HBM per device.

v0:
```python
import functools

import jax
import jax.numpy as jnp
from jax import lax
from jax.experimental import pallas as pl
from jax.experimental.pallas import tpu as pltpu
from jax.sharding import PartitionSpec as P

MESH = pl.DeviceIdType.MESH
F32 = jnp.float32
BF16 = jnp.bfloat16
FORCING_SCALE = (0.1, -0.1, 0.1, 0.1)

SURF, FULL, SECOND, OCEAN, COMP, A1, A2, A3, A4 = 0, 4, 8, 12, 16, 17, 18, 19, 20
SEMS = 21


def split_cat(x):
    hi = x.astype(BF16)
    lo = (x - hi.astype(F32)).astype(BF16)
    return jnp.concatenate([hi, lo], axis=1)


def split_stack(x):
    hi = x.astype(BF16).astype(F32)
    return jnp.concatenate([hi, x - hi], axis=0).astype(BF16)


def dot(a, b):
    return jnp.dot(a, b, preferred_element_type=F32)


def quad(lhs, cat):
    full = dot(lhs, cat)
    return (full[:8, :128] + full[8:, :128]) + (full[:8, 128:] + full[8:, 128:])


def halves(lhs, cat):
    full = dot(lhs, cat)
    return full[:, :128] + full[:, 128:]


def kernel(
    sizes,
    state, remap_a, remap_o, ocean, wet_in,
    diff, e_owner, e_slot, o_owner, o_slot, mixing,
    atmos_out, ocean_out, surf_out,
    S, A, N, MA, MO, MAC, MOC, MAT, MOT, O, ON, W, WN,
    rs_t, rs_b, ks, hs_a, hs_b, hs_l, hs_r,
    rf_t, rf_b, kf, hf_a, hf_b, hf_l, hf_r,
    r2_t, r2_b, k2, h2_a, h2_b, h2_l, h2_r,
    ro_t, ro_b, ko, ho_a, ho_b, ho_l, ho_r,
    X, pieces, MSG, R1, QM, PT, FL, mapped, MSG2, R2, FOR, FORIN,
    TOPC, ANS, B3, OE, OEC, REP, B4, OSV,
    tab_v, tab_s,
    in_sem, out_sem, tab_sem, send, recv,
):
    NC, NX, NY, NF, LEV, NO, OLEV = sizes
    peers = NX * NY
    comp, gx, gy = lax.axis_index("comp"), lax.axis_index("gx"), lax.axis_index("gy")
    me = gx * NY + gy
    pos = comp * NX + gx
    ring = NC * NX
    down, up = lax.rem(pos + 1, ring), lax.rem(pos + ring - 1, ring)
    dev_down = (down // NX, lax.rem(down, NX), gy)
    dev_up = (up // NX, lax.rem(up, NX), gy)
    dev_right = (comp, gx, lax.rem(gy + 1, NY))
    dev_left = (comp, gx, lax.rem(gy + NY - 1, NY))
    sea_down = (comp, lax.rem(gx + 1, NX), gy)
    sea_up = (comp, lax.rem(gx + NX - 1, NX), gy)
    twin = (lax.rem(comp + 1, NC), gx, gy)

    def peer(k):
        px = lax.rem(gx + k // NY, NX)
        py = lax.rem(gy + lax.rem(k, NY), NY)
        return px, py, px * NY + py

    barrier = pltpu.get_barrier_semaphore()

    def greet(k, carry):
        px, py, _ = peer(k)
        pl.semaphore_signal(barrier, inc=1, device_id=(comp, px, py), device_id_type=MESH)
        return carry

    lax.fori_loop(1, peers, greet, 0)
    for other in (dev_down, dev_up, twin):
        pl.semaphore_signal(barrier, inc=1, device_id=other, device_id_type=MESH)

    top_rows = 16 * (LEV - 2)
    loads = [
        pltpu.make_async_copy(state.at[:, pl.ds(top_rows, 32), :], S.at[:, pl.ds(top_rows, 32), :], in_sem.at[0]),
        pltpu.make_async_copy(state.at[:, pl.ds(0, top_rows), :], S.at[:, pl.ds(0, top_rows), :], in_sem.at[1]),
        pltpu.make_async_copy(ocean, O, in_sem.at[2]),
        pltpu.make_async_copy(wet_in, W, in_sem.at[3]),
        pltpu.make_async_copy(remap_a, MA, in_sem.at[4]),
        pltpu.make_async_copy(remap_o, MO, in_sem.at[5]),
    ]
    for load in loads:
        load.start()

    lane16 = lax.broadcasted_iota(jnp.int32, (16, 128), 1)
    row16 = lax.broadcasted_iota(jnp.int32, (16, 128), 0)
    pair16 = lane16 // 2
    even16 = lane16 == pair16 * 2
    sub8 = lax.broadcasted_iota(jnp.int32, (8, 128), 0)

    def places(owner):
        ranks, keys = [], []
        for i in range(16):
            rank = jnp.int32(0)
            for j in range(i):
                rank = rank + (owner[j, 0] == owner[i, 0]).astype(jnp.int32)
            ranks.append(rank)
            keys.append(2 * owner[i, 0] + rank)
        return ranks, keys

    e_rank, e_key = places(e_owner)
    o_rank, o_key = places(o_owner)
    lane8 = lax.broadcasted_iota(jnp.int32, (8, 128), 1)
    table = jnp.zeros((8, 128), jnp.int32)
    for i in range(16):
        table = jnp.where(lane8 == jnp.where(sub8 == 0, e_key[i], o_key[i]), i, table)
    tab_v[...] = table
    tab_copy = pltpu.make_async_copy(tab_v, tab_s, tab_sem.at[0])
    tab_copy.start()

    def remote(src, dst, number, device):
        copy = pltpu.make_async_remote_copy(
            src_ref=src, dst_ref=dst, send_sem=send.at[number], recv_sem=recv.at[number],
            device_id=device, device_id_type=MESH,
        )
        copy.start()
        return copy

    def halo(number, rows_t, rows_b, cols, from_a, from_b, from_l, from_r, below, above):
        return [
            remote(rows_b, from_a, number, below),
            remote(rows_t, from_b, number + 1, above),
            remote(cols, from_l, number + 2, dev_right),
            remote(cols, from_r, number + 3, dev_left),
        ]

    loads[0].wait()
    last = 16 * (LEV - 1)
    packed = jnp.zeros((16, 128), F32)
    for f in range(NF):
        v = S[f, pl.ds(last, 16), :]
        packed = jnp.where(pair16 == f, pltpu.roll(v, 2 * f + 1, 1), packed)
        rs_t[pl.ds(f, 1), :] = v[0:1]
        rs_b[pl.ds(f, 1), :] = v[15:16]
    ks[...] = packed
    pl.semaphore_wait(barrier, peers - 1 + 3)
    surface_halo = halo(SURF, rs_t, rs_b, ks, hs_a, hs_b, hs_l, hs_r, dev_down, dev_up)

    def pack_atmos(src, rows_t, rows_b, cols, f):
        kept = jnp.zeros((16, 128), F32)
        for lev in range(LEV):
            v = src[f, pl.ds(16 * lev, 16), :]
            kept = jnp.where(pair16 == lev, pltpu.roll(v, 2 * lev + 1, 1), kept)
        cols[f] = kept
        rows_t[f, pl.ds(0, LEV), :] = src[f, pl.ds(0, LEV, stride=16), :]
        rows_b[f, pl.ds(0, LEV), :] = src[f, pl.ds(15, LEV, stride=16), :]

    loads[1].wait()

    def pack_first(f, carry):
        pack_atmos(S, rf_t, rf_b, kf, f)
        return carry

    lax.fori_loop(0, NF, pack_first, 0)
    full_halo = halo(FULL, rf_t, rf_b, kf, hf_a, hf_b, hf_l, hf_r, dev_down, dev_up)

    loads[2].wait()
    loads[3].wait()
    planes = NO * OLEV
    lane64 = lax.broadcasted_iota(jnp.int32, (64, 128), 1)
    row64 = lax.broadcasted_iota(jnp.int32, (64, 128), 0)
    pair64 = lane64 // 2
    wet = W[...].astype(F32)
    WN[0] = wet
    kept = jnp.where(pair64 == planes, pltpu.roll(wet, 2 * planes + 1, 1), 0.0)
    ko[...] = kept
    ro_t[pl.ds(planes, 1), :] = wet[0:1]
    ro_b[pl.ds(planes, 1), :] = wet[63:64]

    def pack_ocean(f, carry):
        kept = ko[...]
        for lev in range(OLEV):
            q = f * OLEV + lev
            v = O[pl.ds(pl.multiple_of(q * 64, 64), 64), :]
            kept = jnp.where(pair64 == q, pltpu.roll(v, 2 * q + 1, 1), kept)
        ko[...] = kept
        return carry

    lax.fori_loop(0, NO, pack_ocean, 0)
    ro_t[pl.ds(0, planes), :] = O[pl.ds(0, planes, stride=64), :]
    ro_b[pl.ds(0, planes), :] = O[pl.ds(63, planes, stride=64), :]
    ocean_halo = halo(OCEAN, ro_t, ro_b, ko, ho_a, ho_b, ho_l, ho_r, sea_down, sea_up)

    r128 = lax.broadcasted_iota(jnp.int32, (128, 128), 0)
    lane128 = lax.broadcasted_iota(jnp.int32, (128, 128), 1)
    low128 = lane128 < 64
    labels = jnp.full((128, 128), -1, jnp.int32)
    for i in range(16):
        labels = jnp.where(
            r128 == jnp.where(low128, o_key[i], e_key[i]), jnp.where(low128, o_slot[i], e_slot[i]), labels
        )
    MSG[pl.ds(7, 128, stride=8), :] = labels.astype(F32)

    loads[4].wait()

    def split_a(i, carry):
        MAC[i] = split_cat(MA[i])
        return carry

    lax.fori_loop(0, 16, split_a, 0)

    tab_copy.wait()
    for copy in surface_halo:
        copy.wait_recv()
    kl, kr = hs_l[...], hs_r[...]
    cols = jnp.where(even16, kl, pltpu.roll(kr, 126, 1))
    after = []
    for f in range(NF):
        v = S[f, pl.ds(last, 16), :]
        edge = pltpu.roll(cols, (128 - 2 * f) % 128, 1)
        left = jnp.where(lane16 == 0, edge, pltpu.roll(v, 1, 1))
        right = jnp.where(lane16 == 127, edge, pltpu.roll(v, 127, 1))
        above = jnp.where(row16 == 0, hs_a[pl.ds(f, 1), :], pltpu.roll(v, 1, 0))
        below = jnp.where(row16 == 15, hs_b[pl.ds(f, 1), :], pltpu.roll(v, 15, 0))
        upper = S[f, pl.ds(last - 16, 16), :]
        after.append(v + diff[f] * (above + below + left + right - 4.0 * v) + 0.1 * (upper - v))
    combined = [after[0] - after[4], after[1], after[2], after[3], after[6] + after[7], after[5] + after[8], after[9], after[9]]
    for f in range(8):
        X[pl.ds(16 * f, 16), :] = combined[f]
    for i in range(16):
        pieces[i] = quad(split_stack(X[pl.ds(i, 8, stride=16), :]), MAC[i])

    def pack_pieces(n, carry):
        for m in range(8):
            r = n * 8 + m
            MSG[pl.ds(pl.multiple_of(r * 8, 8), 7), :] = pieces[tab_s[0, r]][0:7]
        return carry

    lax.fori_loop(0, 16, pack_pieces, 0)

    def exchange(number, rows, src, dst_of):
        def step(k, carry):
            px, py, target = peer(k)
            remote(src.at[pl.ds(pl.multiple_of(target * rows, 8), rows), :], dst_of(me), number, (comp, px, py))
            return carry

        lax.fori_loop(1, peers, step, 0)

    def arrived(number, count_ref):
        pltpu.make_async_copy(count_ref, count_ref, recv.at[number]).wait()

    def departed(number, count_ref):
        pltpu.make_async_copy(count_ref, count_ref, send.at[number]).wait()

    mine16 = pl.ds(pl.multiple_of(me * 16, 16), 16)
    mine8 = pl.ds(pl.multiple_of(me * 8, 8), 8)
    exchange(A1, 16, MSG, lambda m: R1.at[pl.ds(pl.multiple_of(m * 16, 16), 16), :])
    R1[mine16, :] = MSG[mine16, :]

    for copy in ocean_halo:
        copy.wait_recv()
    ol, orr = ho_l[...], ho_r[...]
    even64 = lane64 == pair64 * 2
    ho_l[...] = jnp.where(even64, ol, pltpu.roll(orr, 126, 1))

    def around(v, q, edges):
        edge = pltpu.roll(edges, 128 - 2 * q, 1)
        left = jnp.where(lane64 == 0, edge, pltpu.roll(v, 1, 1))
        right = jnp.where(lane64 == 127, edge, pltpu.roll(v, 127, 1))
        above = jnp.where(row64 == 0, ho_a[pl.ds(q, 1), :], pltpu.roll(v, 1, 0))
        below = jnp.where(row64 == 63, ho_b[pl.ds(q, 1), :], pltpu.roll(v, 63, 0))
        return above, below, left, right

    for n, w in enumerate(around(wet, planes, ho_l[...])):
        WN[1 + n] = w

    def sea(f, carry):
        mix = mixing[f]
        base = f * OLEV
        for lev in range(OLEV):
            q = base + lev
            v = O[pl.ds(pl.multiple_of(q * 64, 64), 64), :]
            total = jnp.zeros((64, 128), F32)
            edges = pltpu.roll(ho_l[...], 128 - 2 * q, 1)
            left = jnp.where(lane64 == 0, edges, pltpu.roll(v, 1, 1))
            right = jnp.where(lane64 == 127, edges, pltpu.roll(v, 127, 1))
            above = jnp.where(row64 == 0, ho_a[pl.ds(q, 1), :], pltpu.roll(v, 1, 0))
            below = jnp.where(row64 == 63, ho_b[pl.ds(q, 1), :], pltpu.roll(v, 63, 0))
            total = WN[1] * (above - v) + WN[2] * (below - v) + WN[3] * (left - v) + WN[4] * (right - v)
            upper = v if lev == 0 else O[pl.ds(pl.multiple_of(q * 64 - 64, 64), 64), :]
            lower = v if lev == OLEV - 1 else O[pl.ds(pl.multiple_of(q * 64 + 64, 64), 64), :]
            w = WN[0]
            ON[pl.ds(pl.multiple_of(q * 64, 64), 64), :] = v + w * (
                mix * w * total + 0.1 * (upper + lower - 2.0 * v)
            )
        return carry

    lax.fori_loop(0, NO, sea, 0)

    loads[5].wait()

    def split_o(i, carry):
        MOC[i] = split_cat(MO[i])
        MOT[i] = split_cat(jnp.transpose(MO[i]))
        MAT[i] = split_cat(jnp.transpose(MA[i]))
        return carry

    lax.fori_loop(0, 16, split_o, 0)

    arrived(A1, R1.at[pl.ds(0, 16 * (peers - 1)), :])
    chosen = (R1[pl.ds(7, 128, stride=8), :] == (lane128 - jnp.where(low128, 0, 64)).astype(F32)).astype(F32)
    QM[...] = chosen.astype(BF16)
    PT[...] = jnp.transpose(chosen).astype(BF16)
    fields = [halves(PT[pl.ds(64, 16), :], split_cat(R1[pl.ds(f, 128, stride=8), :])) for f in range(7)]
    heat, salt, east, north, gain, fresh, shape = fields
    speed = jnp.sqrt(east * east + north * north + 0.5)
    flux = [
        speed * heat + gain,
        speed * salt + fresh,
        speed * east * (1.0 + 0.2 * jnp.tanh(shape)),
        speed * north,
    ]
    for g in range(8):
        FL[pl.ds(16 * g, 16), :] = flux[g % 4]
    for j in range(16):
        mapped[j] = quad(split_stack(FL[pl.ds(j, 8, stride=16), :]), MOC[j])

    def pack_mapped(n, carry):
        for m in range(8):
            t = n * 8 + m
            MSG2[pl.ds(pl.multiple_of(t * 8, 8), 8), :] = jnp.where(
                sub8 < 4, mapped[tab_s[1, 2 * t]], mapped[tab_s[1, 2 * t + 1]]
            )
        return carry

    lax.fori_loop(0, peers // 8, pack_mapped, 0)
    exchange(A2, 8, MSG2, lambda m: R2.at[pl.ds(pl.multiple_of(m * 8, 8), 8), :])
    R2[mine8, :] = MSG2[mine8, :]

    for copy in full_halo:
        copy.wait_recv()

    def atmos_field(src, dst, from_a, from_b, from_l, from_r, f):
        d = diff[f]
        both = jnp.where(even16, from_l[f], pltpu.roll(from_r[f], 126, 1))
        for lev in range(LEV):
            v = src[f, pl.ds(16 * lev, 16), :]
            edge = pltpu.roll(both, (128 - 2 * lev) % 128, 1)
            left = jnp.where(lane16 == 0, edge, pltpu.roll(v, 1, 1))
            right = jnp.where(lane16 == 127, edge, pltpu.roll(v, 127, 1))
            above = jnp.where(row16 == 0, from_a[f, pl.ds(lev, 1), :], pltpu.roll(v, 1, 0))
            below = jnp.where(row16 == 15, from_b[f, pl.ds(lev, 1), :], pltpu.roll(v, 15, 0))
            upper = v if lev == 0 else src[f, pl.ds(16 * lev - 16, 16), :]
            lower = v if lev == LEV - 1 else src[f, pl.ds(16 * lev + 16, 16), :]
            dst[f, pl.ds(16 * lev, 16), :] = (
                v + d * (above + below + left + right - 4.0 * v) + 0.1 * (upper + lower - 2.0 * v)
            )

    def first_step(f, carry):
        atmos_field(S, A, hf_a, hf_b, hf_l, hf_r, f)
        pack_atmos(A, r2_t, r2_b, k2, f)
        return carry

    lax.fori_loop(0, NF, first_step, 0)
    second_halo = halo(SECOND, r2_t, r2_b, k2, h2_a, h2_b, h2_l, h2_r, dev_down, dev_up)

    arrived(A2, R2.at[pl.ds(0, 8 * (peers - 1)), :])
    for g in range(NO):
        FOR[pl.ds(64 * g, 64), :] = halves(PT[pl.ds(0, 64), :], split_cat(R2[pl.ds(g, 128, stride=4), :]))
    twin_copy = remote(FOR, FORIN, COMP, twin)
    zero64 = jnp.zeros((64, 256), BF16)
    for g in range(NO):
        TOPC[g, pl.ds(64, 64), :] = zero64
        OEC[g, pl.ds(0, 64), :] = zero64
        OEC[g, pl.ds(64, 64), :] = zero64
    twin_copy.wait_recv()
    for g in range(NO):
        rows = pl.ds(64 * OLEV * g, 64)
        plane = pl.ds(64 * g, 64)
        top = ON[rows, :] + WN[0] * (FORCING_SCALE[g] * (FOR[plane, :] + FORIN[plane, :]))
        ON[rows, :] = top
        TOPC[g, pl.ds(0, 64), :] = split_cat(top)
    for g in range(NO):
        ANS[pl.ds(g, 128, stride=4), :] = halves(QM[...], TOPC[g])
    exchange(A3, 8, ANS, lambda m: B3.at[m])
    B3[me] = ANS[mine8, :]
    ocean_store = pltpu.make_async_copy(ON, ocean_out, out_sem.at[0])
    ocean_store.start()

    for copy in second_halo:
        copy.wait_recv()

    def second_step(f, carry):
        atmos_field(A, N, h2_a, h2_b, h2_l, h2_r, f)
        return carry

    lax.fori_loop(0, NF, second_step, 0)
    atmos_store = pltpu.make_async_copy(N, atmos_out, out_sem.at[1])
    atmos_store.start()

    b3_all = B3.at[pl.ds(0, peers - 1)]
    arrived(A3, b3_all)
    for j in range(16):
        both = quad(split_stack(B3[o_owner[j, 0]]), MOT[j])
        picked = jnp.where(o_rank[j] == 0, both, pltpu.roll(both, 4, 0))
        OE[pl.ds(j, 4, stride=16), :] = picked[0:4]
    for g in range(NO):
        OEC[g, pl.ds(64, 16), :] = split_cat(OE[pl.ds(16 * g, 16), :])
    for g in range(NO):
        REP[pl.ds(g, 128, stride=4), :] = halves(QM[...], OEC[g])
    exchange(A4, 8, REP, lambda m: B4.at[m])
    B4[me] = REP[mine8, :]

    arrived(A4, B4.at[pl.ds(0, peers - 1)])
    for i in range(16):
        both = quad(split_stack(B4[e_owner[i, 0]]), MAT[i])
        picked = jnp.where(e_rank[i] == 0, both, pltpu.roll(both, 4, 0))
        OSV[pl.ds(i, 4, stride=16), :] = picked[0:4]
    surf_store = pltpu.make_async_copy(OSV, surf_out, out_sem.at[2])
    surf_store.start()

    for copy in surface_halo + full_halo + ocean_halo + second_halo + [twin_copy]:
        copy.wait_send()
    departed(A1, MSG.at[pl.ds(0, 16 * (peers - 1)), :])
    departed(A2, MSG2.at[pl.ds(0, 8 * (peers - 1)), :])
    departed(A3, ANS.at[pl.ds(0, 8 * (peers - 1)), :])
    departed(A4, REP.at[pl.ds(0, 8 * (peers - 1)), :])
    ocean_store.wait()
    atmos_store.wait()
    surf_store.wait()


def on_device(
    sizes,
    atmos_state, atmos_diffusion, remap_atmos, exchange_owner, exchange_slot,
    remap_ocean, ocean_owner, ocean_slot, ocean_state, ocean_mixing, wet_mask,
):
    NC, NX, NY, NF, LEV, NO, OLEV = sizes
    peers = NX * NY
    any_ = pl.BlockSpec(memory_space=pl.ANY)
    smem = pl.BlockSpec(memory_space=pltpu.SMEM)

    def vm(*shape, dtype=F32):
        return pltpu.VMEM(shape, dtype)

    halo_atmos = [vm(NF, 24, 128), vm(NF, 24, 128), vm(NF, 16, 128), vm(NF, 24, 128), vm(NF, 24, 128), vm(NF, 16, 128), vm(NF, 16, 128)]
    scratch = (
        [vm(NF, 16 * LEV, 128) for _ in range(3)]
        + [vm(16, 128, 128), vm(16, 128, 128)]
        + [vm(16, 128, 256, dtype=BF16) for _ in range(4)]
        + [vm(NO * OLEV * 64, 128), vm(NO * OLEV * 64, 128), vm(64, 128, dtype=jnp.int32), vm(5, 64, 128)]
        + [vm(16, 128) for _ in range(7)]
        + halo_atmos
        + halo_atmos
        + [vm(40, 128), vm(40, 128), vm(64, 128), vm(40, 128), vm(40, 128), vm(64, 128), vm(64, 128)]
        + [vm(128, 128), vm(16, 8, 128), vm(16 * peers, 128), vm(16 * peers, 128)]
        + [vm(128, 128, dtype=BF16), vm(128, 128, dtype=BF16), vm(128, 128), vm(16, 8, 128)]
        + [vm(8 * peers, 128), vm(8 * peers, 128), vm(256, 128), vm(256, 128)]
        + [vm(NO, 128, 256, dtype=BF16), vm(8 * peers, 128), vm(peers, 8, 128), vm(64, 128)]
        + [vm(NO, 128, 256, dtype=BF16), vm(8 * peers, 128), vm(peers, 8, 128), vm(64, 128)]
        + [vm(8, 128, dtype=jnp.int32), pltpu.SMEM((8, 128), jnp.int32)]
        + [
            pltpu.SemaphoreType.DMA((6,)),
            pltpu.SemaphoreType.DMA((3,)),
            pltpu.SemaphoreType.DMA((1,)),
            pltpu.SemaphoreType.DMA((SEMS,)),
            pltpu.SemaphoreType.DMA((SEMS,)),
        ]
    )
    atmos_next, ocean_next, surface = pl.pallas_call(
        functools.partial(kernel, sizes),
        out_shape=(
            jax.ShapeDtypeStruct((NF, 16 * LEV, 128), F32),
            jax.ShapeDtypeStruct((NO * OLEV * 64, 128), F32),
            jax.ShapeDtypeStruct((64, 128), F32),
        ),
        in_specs=[any_] * 5 + [smem] * 6,
        out_specs=(any_, any_, any_),
        scratch_shapes=scratch,
        compiler_params=pltpu.CompilerParams(
            collective_id=0, has_side_effects=True, vmem_limit_bytes=40 * 1024 * 1024
        ),
    )(
        atmos_state.reshape(NF, 16 * LEV, 128),
        remap_atmos,
        remap_ocean,
        ocean_state.reshape(NO * OLEV * 64, 128),
        wet_mask,
        atmos_diffusion, exchange_owner, exchange_slot, ocean_owner, ocean_slot, ocean_mixing,
    )
    return (
        atmos_next.reshape(NF, LEV, 16, 128),
        ocean_next.reshape(NO, OLEV, 64, 128),
        surface.reshape(NO, 16, 128),
    )


def solution(mesh):
    sizes = (mesh.shape["comp"], mesh.shape["gx"], mesh.shape["gy"], 10, 20, 4, 8)
    in_specs = (
        P(None, None, ("comp", "gx"), "gy"),
        P(),
        P(("comp", "gx", "gy"), None, None),
        P(("comp", "gx", "gy"), None),
        P(("comp", "gx", "gy")),
        P(("comp", "gx", "gy"), None, None),
        P(("comp", "gx", "gy"), None),
        P(("comp", "gx", "gy")),
        P(None, None, "gx", "gy"),
        P(),
        P("gx", "gy"),
    )
    out_specs = (
        P(None, None, ("comp", "gx"), "gy"),
        P(None, None, "gx", "gy"),
        P(None, ("comp", "gx"), "gy"),
    )
    return jax.shard_map(
        functools.partial(on_device, sizes), mesh=mesh, in_specs=in_specs, out_specs=out_specs, check_vma=False
    )
```

profile of v0, /device:TPU:1, one launch (start us, length us, event | category | flops | bytes accessed | tf_op | source)
XLA Modules:
  0.0 66.5 jit_solution(13606707825340126672)
XLA Ops:
  0.6 0.7 %copy.14.e_owner = s32[16,1]{1,0:T(8,128)S(1)} copy(s32[16,1]{0,1:T(1,128)} %param.14) | data formatting | bytes 128 | tf_op args[3]
  1.4 0.7 %copy.15.o_owner = s32[16,1]{1,0:T(8,128)S(1)} copy(s32[16,1]{0,1:T(1,128)} %param.17) | data formatting | bytes 128 | tf_op args[6]
  2.1 0.0 copy-start
  2.1 1.4 %copy-done = f32[10,20,16,128]{3,2,1,0:T(8,128)S(1)} copy-done((f32[10,20,16,128]{3,2,1,0:T(8,128)S(1)}, f32[10,20,16,128]{3,2,1,0:T(8,128)}, u32[]{:S(2)}) %copy-start) | copy-done | bytes 1638424
  3.5 0.0 copy-start.1
  3.5 1.2 %copy-done.1 = f32[16,128,128]{2,1,0:T(8,128)S(1)} copy-done((f32[16,128,128]{2,1,0:T(8,128)S(1)}, f32[16,128,128]{2,1,0:T(8,128)}, u32[]{:S(2)}) %copy-start.1) | copy-done | bytes 1048600
  4.8 0.0 copy-start.2
  4.8 1.2 %copy-done.2 = f32[16,128,128]{2,1,0:T(8,128)S(1)} copy-done((f32[16,128,128]{2,1,0:T(8,128)S(1)}, f32[16,128,128]{2,1,0:T(8,128)}, u32[]{:S(2)}) %copy-start.2) | copy-done | bytes 1048600
  6.0 0.0 copy-start.3
  6.0 1.2 %copy-done.3 = f32[4,8,64,128]{3,2,1,0:T(8,128)S(1)} copy-done((f32[4,8,64,128]{3,2,1,0:T(8,128)S(1)}, f32[4,8,64,128]{3,2,1,0:T(8,128)}, u32[]{:S(2)}) %copy-start.3) | copy-done | bytes 1048600
  7.2 0.0 copy-start.4
  7.2 0.8 %copy-done.4 = s32[64,128]{1,0:T(8,128)S(1)} copy-done((s32[64,128]{1,0:T(8,128)S(1)}, s32[64,128]{1,0:T(8,128)}, u32[]{:S(2)}) %copy-start.4) | copy-done | bytes 32792
  8.0 0.0 copy-start.5
  8.0 0.7 copy-done.5
  8.6 0.0 copy-start.6
  8.6 0.7 copy-done.6
  9.3 0.0 copy-start.7
  9.3 0.7 copy-done.7
  9.9 0.0 copy-start.8
  9.9 0.7 copy-done.8
  10.6 53.2 %shard_map.130 = (f32[10,320,128]{2,1,0:T(8,128)S(1)}, f32[2048,128]{1,0:T(8,128)S(1)}, f32[64,128]{1,0:T(8,128)S(1)}) custom-call(f32[10,320,128]{2,1,0:T(8,128)S(1)} %bitcast.5, f32[16,128,128]{2,1,0:T(8,128)S(1)} %copy-done.1, f32[16,128,128]{2,1,0:T(8,128)S(1)} %copy-done.2, f32[2048,128]{1,0:T(8,128)S(1)} %bitcast.8, s32[64,128]{1,0:T(8,128)S(1)} %copy-done.4, ...), custom_call_target="tpu_custom_call" | custom-call | tf_op jit(solution)/shard_map/pallas_call | solution.py:477
  63.7 1.2 %copy.19 = f32[10,20,16,128]{3,2,1,0:T(8,128)} copy(f32[10,20,16,128]{3,2,1,0:T(8,128)S(1)} %bitcast.6) | data formatting | bytes 3276800
  64.9 1.0 %copy.20 = f32[4,8,64,128]{3,2,1,0:T(8,128)} copy(f32[4,8,64,128]{3,2,1,0:T(8,128)S(1)} %bitcast.7) | data formatting | bytes 2097152
  65.9 0.6 copy.21
Async XLA Ops:
  2.1 1.4 %copy-start = (f32[10,20,16,128]{3,2,1,0:T(8,128)S(1)}, f32[10,20,16,128]{3,2,1,0:T(8,128)}, u32[]{:S(2)}) copy-start(f32[10,20,16,128]{3,2,1,0:T(8,128)} %param.11) | copy-start | bytes 4915204
  3.5 1.2 %copy-start.1 = (f32[16,128,128]{2,1,0:T(8,128)S(1)}, f32[16,128,128]{2,1,0:T(8,128)}, u32[]{:S(2)}) copy-start(f32[16,128,128]{2,1,0:T(8,128)} %remap_a.1) | copy-start | bytes 3145732
  4.8 1.2 %copy-start.2 = (f32[16,128,128]{2,1,0:T(8,128)S(1)}, f32[16,128,128]{2,1,0:T(8,128)}, u32[]{:S(2)}) copy-start(f32[16,128,128]{2,1,0:T(8,128)} %remap_o.1) | copy-start | bytes 3145732
  6.0 1.2 %copy-start.3 = (f32[4,8,64,128]{3,2,1,0:T(8,128)S(1)}, f32[4,8,64,128]{3,2,1,0:T(8,128)}, u32[]{:S(2)}) copy-start(f32[4,8,64,128]{3,2,1,0:T(8,128)} %param.19) | copy-start | bytes 3145732
  7.2 0.8 %copy-start.4 = (s32[64,128]{1,0:T(8,128)S(1)}, s32[64,128]{1,0:T(8,128)}, u32[]{:S(2)}) copy-start(s32[64,128]{1,0:T(8,128)} %wet_in.1) | copy-start | bytes 98308
  8.0 0.7 copy-start.5
  8.6 0.7 copy-start.6
  9.3 0.7 copy-start.7
  9.9 0.7 copy-start.8
where the time goes:
time: 66.9 us; the launch traced here: 66.5 us
  Pallas kernels  53.2 us (80%)
  local copies, waits for them, and re-layouts  12.7 us (19%)
    pallas_call x1, Pallas kernels, on_device(): pl.pallas_call(functools.partial(kernel, sizes), out_shape=(jax.ShapeDtyp...  53.2 us
    unnamed x23, local copies, waits for them, and re-layouts  12.7 us

commit v1 on v0

--- a/solution.py
+++ b/solution.py
@@ -44,7 +44,7 @@
 def kernel(
     sizes,
     state, remap_a, remap_o, ocean, wet_in,
-    diff, e_owner, e_slot, o_owner, o_slot, mixing,
+    diff_in, e_owner_in, e_slot_in, o_owner_in, o_slot_in, mixing_in,
     atmos_out, ocean_out, surf_out,
     S, A, N, MA, MO, MAC, MOC, MAT, MOT, O, ON, W, WN,
     rs_t, rs_b, ks, hs_a, hs_b, hs_l, hs_r,
@@ -53,6 +53,7 @@
     ro_t, ro_b, ko, ho_a, ho_b, ho_l, ho_r,
     X, pieces, MSG, R1, QM, PT, FL, mapped, MSG2, R2, FOR, FORIN,
     TOPC, ANS, B3, OE, OEC, REP, B4, OSV,
+    diff, e_owner, e_slot, o_owner, o_slot, mixing,
     tab_v, tab_s,
     in_sem, out_sem, tab_sem, send, recv,
 ):
@@ -96,7 +97,14 @@
         pltpu.make_async_copy(remap_a, MA, in_sem.at[4]),
         pltpu.make_async_copy(remap_o, MO, in_sem.at[5]),
     ]
-    for load in loads:
+    small = [
+        pltpu.make_async_copy(src, dst, in_sem.at[6 + n])
+        for n, (src, dst) in enumerate([
+            (e_owner_in, e_owner), (o_owner_in, o_owner), (e_slot_in, e_slot), (o_slot_in, o_slot),
+            (diff_in, diff), (mixing_in, mixing),
+        ])
+    ]
+    for load in small + loads:
         load.start()
 
     lane16 = lax.broadcasted_iota(jnp.int32, (16, 128), 1)
@@ -104,26 +112,6 @@
     pair16 = lane16 // 2
     even16 = lane16 == pair16 * 2
     sub8 = lax.broadcasted_iota(jnp.int32, (8, 128), 0)
-
-    def places(owner):
-        ranks, keys = [], []
-        for i in range(16):
-            rank = jnp.int32(0)
-            for j in range(i):
-                rank = rank + (owner[j, 0] == owner[i, 0]).astype(jnp.int32)
-            ranks.append(rank)
-            keys.append(2 * owner[i, 0] + rank)
-        return ranks, keys
-
-    e_rank, e_key = places(e_owner)
-    o_rank, o_key = places(o_owner)
-    lane8 = lax.broadcasted_iota(jnp.int32, (8, 128), 1)
-    table = jnp.zeros((8, 128), jnp.int32)
-    for i in range(16):
-        table = jnp.where(lane8 == jnp.where(sub8 == 0, e_key[i], o_key[i]), i, table)
-    tab_v[...] = table
-    tab_copy = pltpu.make_async_copy(tab_v, tab_s, tab_sem.at[0])
-    tab_copy.start()
 
     def remote(src, dst, number, device):
         copy = pltpu.make_async_remote_copy(
@@ -152,6 +140,28 @@
     ks[...] = packed
     pl.semaphore_wait(barrier, peers - 1 + 3)
     surface_halo = halo(SURF, rs_t, rs_b, ks, hs_a, hs_b, hs_l, hs_r, dev_down, dev_up)
+
+    def places(owner):
+        ranks, keys = [], []
+        for i in range(16):
+            rank = jnp.int32(0)
+            for j in range(i):
+                rank = rank + (owner[j] == owner[i]).astype(jnp.int32)
+            ranks.append(rank)
+            keys.append(2 * owner[i] + rank)
+        return ranks, keys
+
+    for load in small:
+        load.wait()
+    e_rank, e_key = places(e_owner)
+    o_rank, o_key = places(o_owner)
+    lane8 = lax.broadcasted_iota(jnp.int32, (8, 128), 1)
+    table = jnp.zeros((8, 128), jnp.int32)
+    for i in range(16):
+        table = jnp.where(lane8 == jnp.where(sub8 == 0, e_key[i], o_key[i]), i, table)
+    tab_v[...] = table
+    tab_copy = pltpu.make_async_copy(tab_v, tab_s, tab_sem.at[0])
+    tab_copy.start()
 
     def pack_atmos(src, rows_t, rows_b, cols, f):
         kept = jnp.zeros((16, 128), F32)
@@ -408,7 +418,7 @@
     b3_all = B3.at[pl.ds(0, peers - 1)]
     arrived(A3, b3_all)
     for j in range(16):
-        both = quad(split_stack(B3[o_owner[j, 0]]), MOT[j])
+        both = quad(split_stack(B3[o_owner[j]]), MOT[j])
         picked = jnp.where(o_rank[j] == 0, both, pltpu.roll(both, 4, 0))
         OE[pl.ds(j, 4, stride=16), :] = picked[0:4]
     for g in range(NO):
@@ -420,7 +430,7 @@
 
     arrived(A4, B4.at[pl.ds(0, peers - 1)])
     for i in range(16):
-        both = quad(split_stack(B4[e_owner[i, 0]]), MAT[i])
+        both = quad(split_stack(B4[e_owner[i]]), MAT[i])
         picked = jnp.where(e_rank[i] == 0, both, pltpu.roll(both, 4, 0))
         OSV[pl.ds(i, 4, stride=16), :] = picked[0:4]
     surf_store = pltpu.make_async_copy(OSV, surf_out, out_sem.at[2])
@@ -444,8 +454,7 @@
 ):
     NC, NX, NY, NF, LEV, NO, OLEV = sizes
     peers = NX * NY
-    any_ = pl.BlockSpec(memory_space=pl.ANY)
-    smem = pl.BlockSpec(memory_space=pltpu.SMEM)
+    hbm = pl.BlockSpec(memory_space=pltpu.HBM)
 
     def vm(*shape, dtype=F32):
         return pltpu.VMEM(shape, dtype)
@@ -465,9 +474,10 @@
         + [vm(8 * peers, 128), vm(8 * peers, 128), vm(256, 128), vm(256, 128)]
         + [vm(NO, 128, 256, dtype=BF16), vm(8 * peers, 128), vm(peers, 8, 128), vm(64, 128)]
         + [vm(NO, 128, 256, dtype=BF16), vm(8 * peers, 128), vm(peers, 8, 128), vm(64, 128)]
+        + [pltpu.SMEM((NF,), F32)] + [pltpu.SMEM((16,), jnp.int32) for _ in range(4)] + [pltpu.SMEM((NO,), F32)]
         + [vm(8, 128, dtype=jnp.int32), pltpu.SMEM((8, 128), jnp.int32)]
         + [
-            pltpu.SemaphoreType.DMA((6,)),
+            pltpu.SemaphoreType.DMA((12,)),
             pltpu.SemaphoreType.DMA((3,)),
             pltpu.SemaphoreType.DMA((1,)),
             pltpu.SemaphoreType.DMA((SEMS,)),
@@ -481,11 +491,11 @@
             jax.ShapeDtypeStruct((NO * OLEV * 64, 128), F32),
             jax.ShapeDtypeStruct((64, 128), F32),
         ),
-        in_specs=[any_] * 5 + [smem] * 6,
-        out_specs=(any_, any_, any_),
+        in_specs=[hbm] * 11,
+        out_specs=(hbm, hbm, hbm),
         scratch_shapes=scratch,
         compiler_params=pltpu.CompilerParams(
-            collective_id=0, has_side_effects=True, vmem_limit_bytes=40 * 1024 * 1024
+            collective_id=0, has_side_effects=True, vmem_limit_bytes=62 * 1024 * 1024
         ),
     )(
         atmos_state.reshape(NF, 16 * LEV, 128),
@@ -493,7 +503,7 @@
         remap_ocean,
         ocean_state.reshape(NO * OLEV * 64, 128),
         wet_mask,
-        atmos_diffusion, exchange_owner, exchange_slot, ocean_owner, ocean_slot, ocean_mixing,
+        atmos_diffusion, exchange_owner.reshape(16), exchange_slot, ocean_owner.reshape(16), ocean_slot, ocean_mixing,
     )
     return (
         atmos_next.reshape(NF, LEV, 16, 128),

time: 66.9 us -> 58.6 us (0.88)
  local copies, waits for them, and re-layouts: 12.7 us -> 4.4 us
    unnamed x23 -> x7, local copies, waits for them, and re-layouts: 12.7 us -> 4.4 us
where the time goes in v1:
time: 58.6 us; the launch traced here: 58.5 us
  Pallas kernels  53.4 us (91%)
  local copies, waits for them, and re-layouts  4.4 us (8%)
  between operations  0.65 us (1%)
    pallas_call x1, Pallas kernels, on_device(): pl.pallas_call(functools.partial(kernel, sizes), out_shape=(jax.ShapeDtyp...  53.4 us
    unnamed x7, local copies, waits for them, and re-layouts  4.4 us

profile of v1, /device:TPU:1, one launch (start us, length us, event | category | flops | bytes accessed | tf_op | source)
XLA Modules:
  0.0 58.5 jit_solution(8135010704499404951)
XLA Ops:
  0.6 53.4 %shard_map.130 = (f32[10,320,128]{2,1,0:T(8,128)}, f32[2048,128]{1,0:T(8,128)}, f32[64,128]{1,0:T(8,128)}) custom-call(f32[10,320,128]{2,1,0:T(8,128)} %bitcast.7, f32[16,128,128]{2,1,0:T(8,128)} %remap_a.1, f32[16,128,128]{2,1,0:T(8,128)} %remap_o.1, f32[2048,128]{1,0:T(8,128)} %bitcast.9, s32[64,128]{1,0:T(8,128)} %wet_in.1, f32[10]{0:T(128)} %diff_in.1, ...), custom_call_target="tpu_custom_call" | custom-call | tf_op jit(solution)/shard_map/pallas_call | solution.py:487
  54.0 0.0 copy-start
  54.1 2.8 %copy.17 = f32[10,20,16,128]{3,2,1,0:T(8,128)} copy(f32[10,20,16,128]{3,2,1,0:T(8,128)} %bitcast.8) | data formatting | bytes 3276800
  56.9 0.0 copy-done
  56.9 0.0 copy-start.1
  56.9 1.0 %copy.18 = f32[4,8,64,128]{3,2,1,0:T(8,128)} copy(f32[4,8,64,128]{3,2,1,0:T(8,128)S(1)} %bitcast.10) | data formatting | bytes 2097152
  57.8 0.0 copy-done.1
  57.8 0.6 %copy.19 = f32[4,16,128]{2,1,0:T(8,128)} copy(f32[4,16,128]{2,1,0:T(8,128)S(1)} %bitcast.11) | data formatting | bytes 65536
Async XLA Ops:
  54.0 2.8 %copy-start = (f32[2048,128]{1,0:T(8,128)S(1)}, f32[2048,128]{1,0:T(8,128)}, u32[]{:S(2)}) copy-start(f32[2048,128]{1,0:T(8,128)} %get-tuple-element.7) | copy-start | bytes 3145732
  56.9 1.0 %copy-start.1 = (f32[64,128]{1,0:T(8,128)S(1)}, f32[64,128]{1,0:T(8,128)}, u32[]{:S(2)}) copy-start(f32[64,128]{1,0:T(8,128)} %get-tuple-element.8) | copy-start | bytes 98308

commit v2 on v1

--- a/solution.py
+++ b/solution.py
@@ -14,6 +14,18 @@
 
 SURF, FULL, SECOND, OCEAN, COMP, A1, A2, A3, A4 = 0, 4, 8, 12, 16, 17, 18, 19, 20
 SEMS = 21
+
+
+def far_first(nx, ny):
+    def way(n, offset, flip):
+        total = 0
+        for at in range(n):
+            to = (at + offset) % n
+            ahead = (to - at) % 4
+            total += min(ahead, 4 - ahead) + flip * (to // 4 != at // 4)
+        return total / n
+
+    return sorted(range(1, nx * ny), key=lambda k: (-way(nx, k // ny, 2) - way(ny, k % ny, 1), k))
 
 
 def split_cat(x):
@@ -172,15 +184,6 @@
         rows_t[f, pl.ds(0, LEV), :] = src[f, pl.ds(0, LEV, stride=16), :]
         rows_b[f, pl.ds(0, LEV), :] = src[f, pl.ds(15, LEV, stride=16), :]
 
-    loads[1].wait()
-
-    def pack_first(f, carry):
-        pack_atmos(S, rf_t, rf_b, kf, f)
-        return carry
-
-    lax.fori_loop(0, NF, pack_first, 0)
-    full_halo = halo(FULL, rf_t, rf_b, kf, hf_a, hf_b, hf_l, hf_r, dev_down, dev_up)
-
     loads[2].wait()
     loads[3].wait()
     planes = NO * OLEV
@@ -261,7 +264,8 @@
             remote(src.at[pl.ds(pl.multiple_of(target * rows, 8), rows), :], dst_of(me), number, (comp, px, py))
             return carry
 
-        lax.fori_loop(1, peers, step, 0)
+        for k in far_first(NX, NY):
+            step(k, 0)
 
     def arrived(number, count_ref):
         pltpu.make_async_copy(count_ref, count_ref, recv.at[number]).wait()
@@ -273,6 +277,15 @@
     mine8 = pl.ds(pl.multiple_of(me * 8, 8), 8)
     exchange(A1, 16, MSG, lambda m: R1.at[pl.ds(pl.multiple_of(m * 16, 16), 16), :])
     R1[mine16, :] = MSG[mine16, :]
+
+    loads[1].wait()
+
+    def pack_first(f, carry):
+        pack_atmos(S, rf_t, rf_b, kf, f)
+        return carry
+
+    lax.fori_loop(0, NF, pack_first, 0)
+    full_halo = halo(FULL, rf_t, rf_b, kf, hf_a, hf_b, hf_l, hf_r, dev_down, dev_up)
 
     for copy in ocean_halo:
         copy.wait_recv()
@@ -379,7 +392,6 @@
         return carry
 
     lax.fori_loop(0, NF, first_step, 0)
-    second_halo = halo(SECOND, r2_t, r2_b, k2, h2_a, h2_b, h2_l, h2_r, dev_down, dev_up)
 
     arrived(A2, R2.at[pl.ds(0, 8 * (peers - 1)), :])
     for g in range(NO):
@@ -401,19 +413,9 @@
         ANS[pl.ds(g, 128, stride=4), :] = halves(QM[...], TOPC[g])
     exchange(A3, 8, ANS, lambda m: B3.at[m])
     B3[me] = ANS[mine8, :]
+    second_halo = halo(SECOND, r2_t, r2_b, k2, h2_a, h2_b, h2_l, h2_r, dev_down, dev_up)
     ocean_store = pltpu.make_async_copy(ON, ocean_out, out_sem.at[0])
     ocean_store.start()
-
-    for copy in second_halo:
-        copy.wait_recv()
-
-    def second_step(f, carry):
-        atmos_field(A, N, h2_a, h2_b, h2_l, h2_r, f)
-        return carry
-
-    lax.fori_loop(0, NF, second_step, 0)
-    atmos_store = pltpu.make_async_copy(N, atmos_out, out_sem.at[1])
-    atmos_store.start()
 
     b3_all = B3.at[pl.ds(0, peers - 1)]
     arrived(A3, b3_all)
@@ -428,6 +430,17 @@
     exchange(A4, 8, REP, lambda m: B4.at[m])
     B4[me] = REP[mine8, :]
 
+    for copy in second_halo:
+        copy.wait_recv()
+
+    def second_step(f, carry):
+        atmos_field(A, N, h2_a, h2_b, h2_l, h2_r, f)
+        return carry
+
+    lax.fori_loop(0, NF, second_step, 0)
+    atmos_store = pltpu.make_async_copy(N, atmos_out, out_sem.at[1])
+    atmos_store.start()
+
     arrived(A4, B4.at[pl.ds(0, peers - 1)])
     for i in range(16):
         both = quad(split_stack(B4[e_owner[i]]), MAT[i])
@@ -447,6 +460,14 @@
     surf_store.wait()
 
 
+def hand_out(a, b, c, a_out, b_out, c_out, sem):
+    copies = [pltpu.make_async_copy(x, y, sem.at[n]) for n, (x, y) in enumerate([(a, a_out), (b, b_out), (c, c_out)])]
+    for copy in copies:
+        copy.start()
+    for copy in copies:
+        copy.wait()
+
+
 def on_device(
     sizes,
     atmos_state, atmos_diffusion, remap_atmos, exchange_owner, exchange_slot,
@@ -455,6 +476,7 @@
     NC, NX, NY, NF, LEV, NO, OLEV = sizes
     peers = NX * NY
     hbm = pl.BlockSpec(memory_space=pltpu.HBM)
+    any_ = pl.BlockSpec(memory_space=pl.ANY)
 
     def vm(*shape, dtype=F32):
         return pltpu.VMEM(shape, dtype)
@@ -492,19 +514,28 @@
             jax.ShapeDtypeStruct((64, 128), F32),
         ),
         in_specs=[hbm] * 11,
-        out_specs=(hbm, hbm, hbm),
+        out_specs=(any_, any_, any_),
         scratch_shapes=scratch,
         compiler_params=pltpu.CompilerParams(
-            collective_id=0, has_side_effects=True, vmem_limit_bytes=62 * 1024 * 1024
+            collective_id=0, has_side_effects=True, vmem_limit_bytes=40 * 1024 * 1024
         ),
-    )(
+    )(*(pltpu.with_memory_space_constraint(x, pltpu.HBM) for x in (
         atmos_state.reshape(NF, 16 * LEV, 128),
         remap_atmos,
         remap_ocean,
         ocean_state.reshape(NO * OLEV * 64, 128),
         wet_mask,
         atmos_diffusion, exchange_owner.reshape(16), exchange_slot, ocean_owner.reshape(16), ocean_slot, ocean_mixing,
-    )
+    )))
+    results = (atmos_next, ocean_next, surface)
+    atmos_next, ocean_next, surface = pl.pallas_call(
+        hand_out,
+        out_shape=tuple(jax.ShapeDtypeStruct(x.shape, x.dtype) for x in results),
+        in_specs=[any_] * 3,
+        out_specs=(hbm, hbm, hbm),
+        scratch_shapes=[pltpu.SemaphoreType.DMA((3,))],
+        compiler_params=pltpu.CompilerParams(vmem_limit_bytes=1024 * 1024),
+    )(*results)
     return (
         atmos_next.reshape(NF, LEV, 16, 128),
         ocean_next.reshape(NO, OLEV, 64, 128),

time: 58.6 us -> 51.9 us (0.89)
  local copies, waits for them, and re-layouts: 4.4 us -> 0 us
  Pallas kernels: 53.4 us -> 51.1 us
    unnamed x7 -> x0, local copies, waits for them, and re-layouts: 4.4 us -> none
    pallas_call x1, Pallas kernels: 53.4 us -> 49.6 us  [on_device(): pl.pallas_call(functools.partial(kernel, sizes), out_shape=(jax.ShapeDtyp...]
    pallas_call x0 -> x1, Pallas kernels: none -> 1.54 us  [on_device(): pl.pallas_call(hand_out, out_shape=tuple((jax.ShapeDtypeStruct(x.shape, x...]
where the time goes in v2:
time: 51.9 us; the launch traced here: 51.8 us
  Pallas kernels  51.1 us (98%)
  between operations  0.64 us (1%)
    pallas_call x1, Pallas kernels, on_device(): pl.pallas_call(functools.partial(kernel, sizes), out_shape=(jax.ShapeDtyp...  49.6 us
    pallas_call x1, Pallas kernels, on_device(): pl.pallas_call(hand_out, out_shape=tuple((jax.ShapeDtypeStruct(x.shape, x...  1.54 us

profile of v2, /device:TPU:1, one launch (start us, length us, event | category | flops | bytes accessed | tf_op | source)
XLA Modules:
  0.0 51.8 jit_solution(64416492967935521)
XLA Ops:
  0.6 49.6 %shard_map.130 = (f32[10,320,128]{2,1,0:T(8,128)S(1)}, f32[2048,128]{1,0:T(8,128)S(1)}, f32[64,128]{1,0:T(8,128)S(1)}) custom-call(f32[10,320,128]{2,1,0:T(8,128)} %bitcast.7, f32[16,128,128]{2,1,0:T(8,128)} %remap_a.1, f32[16,128,128]{2,1,0:T(8,128)} %remap_o.1, f32[2048,128]{1,0:T(8,128)} %bitcast.8, s32[64,128]{1,0:T(8,128)} %wet_in.1, f32[10]{0:T(128)} %diff_in.1, ...), custom_call_target="tpu_custom_call" | custom-call | tf_op jit(solution)/shard_map/pallas_call | solution.py:509
  50.2 1.5 %shard_map.131 = (f32[10,320,128]{2,1,0:T(8,128)}, f32[2048,128]{1,0:T(8,128)}, f32[64,128]{1,0:T(8,128)}) custom-call(f32[10,320,128]{2,1,0:T(8,128)S(1)} %get-tuple-element.9.a, f32[2048,128]{1,0:T(8,128)S(1)} %get-tuple-element.10.b, f32[64,128]{1,0:T(8,128)S(1)} %get-tuple-element.11.c), custom_call_target="tpu_custom_call" | custom-call | tf_op jit(solution)/shard_map/pallas_call | solution.py:531

commit v3 on v2

--- a/solution.py
+++ b/solution.py
@@ -67,7 +67,7 @@
     TOPC, ANS, B3, OE, OEC, REP, B4, OSV,
     diff, e_owner, e_slot, o_owner, o_slot, mixing,
     tab_v, tab_s,
-    in_sem, out_sem, tab_sem, send, recv,
+    in_sem, out_sem, tab_sem, send, recv, row_here,
 ):
     NC, NX, NY, NF, LEV, NO, OLEV = sizes
     peers = NX * NY
@@ -91,13 +91,10 @@
 
     barrier = pltpu.get_barrier_semaphore()
 
-    def greet(k, carry):
-        px, py, _ = peer(k)
-        pl.semaphore_signal(barrier, inc=1, device_id=(comp, px, py), device_id_type=MESH)
-        return carry
-
-    lax.fori_loop(1, peers, greet, 0)
-    for other in (dev_down, dev_up, twin):
+    row_peers = [(comp, gx, lax.rem(gy + b, NY)) for b in range(1, NY)]
+    column_peers = [(comp, lax.rem(gx + a, NX), gy) for a in range(1, NX)]
+    greeted = row_peers + column_peers + [dev_down, dev_up, twin]
+    for other in greeted:
         pl.semaphore_signal(barrier, inc=1, device_id=other, device_id_type=MESH)
 
     top_rows = 16 * (LEV - 2)
@@ -150,8 +147,10 @@
         rs_t[pl.ds(f, 1), :] = v[0:1]
         rs_b[pl.ds(f, 1), :] = v[15:16]
     ks[...] = packed
-    pl.semaphore_wait(barrier, peers - 1 + 3)
+    pl.semaphore_wait(barrier, len(greeted))
     surface_halo = halo(SURF, rs_t, rs_b, ks, hs_a, hs_b, hs_l, hs_r, dev_down, dev_up)
+    for other in column_peers:
+        pl.semaphore_signal(row_here.at[0], inc=1, device_id=other, device_id_type=MESH)
 
     def places(owner):
         ranks, keys = [], []
@@ -275,6 +274,7 @@
 
     mine16 = pl.ds(pl.multiple_of(me * 16, 16), 16)
     mine8 = pl.ds(pl.multiple_of(me * 8, 8), 8)
+    pl.semaphore_wait(row_here.at[0], NX - 1)
     exchange(A1, 16, MSG, lambda m: R1.at[pl.ds(pl.multiple_of(m * 16, 16), 16), :])
     R1[mine16, :] = MSG[mine16, :]
 
@@ -504,6 +504,7 @@
             pltpu.SemaphoreType.DMA((1,)),
             pltpu.SemaphoreType.DMA((SEMS,)),
             pltpu.SemaphoreType.DMA((SEMS,)),
+            pltpu.SemaphoreType.REGULAR((1,)),
         ]
     )
     atmos_next, ocean_next, surface = pl.pallas_call(

time: 51.9 us -> 50.9 us (0.981)
  Pallas kernels: 51.1 us -> 50.1 us
    pallas_call x1, Pallas kernels: 49.6 us -> 48.6 us  [on_device(): pl.pallas_call(functools.partial(kernel, sizes), out_shape=(jax.ShapeDtyp...]
where the time goes in v3:
time: 50.9 us; the launch traced here: 50.8 us
  Pallas kernels  50.1 us (98%)
  between operations  0.64 us (1%)
    pallas_call x1, Pallas kernels, on_device(): pl.pallas_call(functools.partial(kernel, sizes), out_shape=(jax.ShapeDtyp...  48.6 us
    pallas_call x1, Pallas kernels, on_device(): pl.pallas_call(hand_out, out_shape=tuple((jax.ShapeDtypeStruct(x.shape, x...  1.54 us

profile of v3, /device:TPU:1, one launch (start us, length us, event | category | flops | bytes accessed | tf_op | source)
XLA Modules:
  0.0 50.8 jit_solution(11237035346439379530)
XLA Ops:
  0.6 48.6 %shard_map.130 = (f32[10,320,128]{2,1,0:T(8,128)S(1)}, f32[2048,128]{1,0:T(8,128)S(1)}, f32[64,128]{1,0:T(8,128)S(1)}) custom-call(f32[10,320,128]{2,1,0:T(8,128)} %bitcast.7, f32[16,128,128]{2,1,0:T(8,128)} %remap_a.1, f32[16,128,128]{2,1,0:T(8,128)} %remap_o.1, f32[2048,128]{1,0:T(8,128)} %bitcast.8, s32[64,128]{1,0:T(8,128)} %wet_in.1, f32[10]{0:T(128)} %diff_in.1, ...), custom_call_target="tpu_custom_call" | custom-call | tf_op jit(solution)/shard_map/pallas_call | solution.py:510
  49.2 1.5 %shard_map.131 = (f32[10,320,128]{2,1,0:T(8,128)}, f32[2048,128]{1,0:T(8,128)}, f32[64,128]{1,0:T(8,128)}) custom-call(f32[10,320,128]{2,1,0:T(8,128)S(1)} %get-tuple-element.9.a, f32[2048,128]{1,0:T(8,128)S(1)} %get-tuple-element.10.b, f32[64,128]{1,0:T(8,128)S(1)} %get-tuple-element.11.c), custom_call_target="tpu_custom_call" | custom-call | tf_op jit(solution)/shard_map/pallas_call | solution.py:532

commit v4 on v3

--- a/solution.py
+++ b/solution.py
@@ -12,8 +12,8 @@
 BF16 = jnp.bfloat16
 FORCING_SCALE = (0.1, -0.1, 0.1, 0.1)
 
-SURF, FULL, SECOND, OCEAN, COMP, A1, A2, A3, A4 = 0, 4, 8, 12, 16, 17, 18, 19, 20
-SEMS = 21
+SURF, FULL, SECOND, OCEAN, COMP, A1, A2, A3, A4, LABELS = 0, 4, 8, 12, 16, 17, 18, 19, 20, 21
+SEMS = 22
 
 
 def far_first(nx, ny):
@@ -46,6 +46,15 @@
 def quad(lhs, cat):
     full = dot(lhs, cat)
     return (full[:8, :128] + full[8:, :128]) + (full[:8, 128:] + full[8:, 128:])
+
+
+def both_ranks(ref, first, apart, stride):
+    return jnp.concatenate([ref[pl.ds(first + apart * c, 64, stride=stride), :] for c in range(2)], axis=0)
+
+
+def put_ranks(ref, g, rows):
+    for c in range(2):
+        ref[pl.ds(g + 4 * c, 64, stride=8), :] = rows[64 * c : 64 * c + 64]
 
 
 def halves(lhs, cat):
@@ -63,7 +72,7 @@
     rf_t, rf_b, kf, hf_a, hf_b, hf_l, hf_r,
     r2_t, r2_b, k2, h2_a, h2_b, h2_l, h2_r,
     ro_t, ro_b, ko, ho_a, ho_b, ho_l, ho_r,
-    X, pieces, MSG, R1, QM, PT, FL, mapped, MSG2, R2, FOR, FORIN,
+    NOTE, NOTES, X, pieces, shifted, MSG, R1, QM, PT, FL, mapped, MSG2, R2, FOR, FORIN,
     TOPC, ANS, B3, OE, OEC, REP, B4, OSV,
     diff, e_owner, e_slot, o_owner, o_slot, mixing,
     tab_v, tab_s,
@@ -131,6 +140,9 @@
         return copy
 
     def halo(number, rows_t, rows_b, cols, from_a, from_b, from_l, from_r, below, above):
+        if len(rows_b.shape) == 3:
+            used = pl.ds(0, LEV)
+            rows_t, rows_b, from_a, from_b = (ref.at[:, used, :] for ref in (rows_t, rows_b, from_a, from_b))
         return [
             remote(rows_b, from_a, number, below),
             remote(rows_t, from_b, number + 1, above),
@@ -210,16 +222,6 @@
     ro_b[pl.ds(0, planes), :] = O[pl.ds(63, planes, stride=64), :]
     ocean_halo = halo(OCEAN, ro_t, ro_b, ko, ho_a, ho_b, ho_l, ho_r, sea_down, sea_up)
 
-    r128 = lax.broadcasted_iota(jnp.int32, (128, 128), 0)
-    lane128 = lax.broadcasted_iota(jnp.int32, (128, 128), 1)
-    low128 = lane128 < 64
-    labels = jnp.full((128, 128), -1, jnp.int32)
-    for i in range(16):
-        labels = jnp.where(
-            r128 == jnp.where(low128, o_key[i], e_key[i]), jnp.where(low128, o_slot[i], e_slot[i]), labels
-        )
-    MSG[pl.ds(7, 128, stride=8), :] = labels.astype(F32)
-
     loads[4].wait()
 
     def split_a(i, carry):
@@ -227,6 +229,18 @@
         return carry
 
     lax.fori_loop(0, 16, split_a, 0)
+
+    lane1 = lax.broadcasted_iota(jnp.int32, (1, 128), 1)
+    row = jnp.zeros((1, 128), jnp.int32)
+    for i in range(16):
+        for at, value in ((0, e_key[i]), (16, e_slot[i] + 1), (32, o_key[i]), (48, o_slot[i] + 1)):
+            row = jnp.where(lane1 == at + i, value, row)
+    NOTE[0] = row.astype(F32)
+    NOTES[me] = row.astype(F32)
+    pl.semaphore_wait(row_here.at[0], NX - 1)
+    for k in far_first(NX, NY):
+        px, py, _ = peer(k)
+        remote(NOTE.at[0], NOTES.at[me], LABELS, (comp, px, py))
 
     tab_copy.wait()
     for copy in surface_halo:
@@ -247,20 +261,24 @@
     for f in range(8):
         X[pl.ds(16 * f, 16), :] = combined[f]
     for i in range(16):
-        pieces[i] = quad(split_stack(X[pl.ds(i, 8, stride=16), :]), MAC[i])
+        piece = quad(split_stack(X[pl.ds(i, 8, stride=16), :]), MAC[i])
+        pieces[i] = piece
+        shifted[i] = pltpu.roll(piece, 7, 0)
 
     def pack_pieces(n, carry):
-        for m in range(8):
-            r = n * 8 + m
-            MSG[pl.ds(pl.multiple_of(r * 8, 8), 7), :] = pieces[tab_s[0, r]][0:7]
+        for m in range(4):
+            t = n * 4 + m
+            one, two = pieces[tab_s[0, 2 * t]], shifted[tab_s[0, 2 * t + 1]]
+            MSG[pl.ds(pl.multiple_of(t * 16, 16), 8), :] = jnp.where(sub8 < 7, one, two)
+            MSG[pl.ds(pl.multiple_of(t * 16 + 8, 8), 8), :] = two
         return carry
 
     lax.fori_loop(0, 16, pack_pieces, 0)
 
-    def exchange(number, rows, src, dst_of):
+    def exchange(number, rows, sent, src, dst_of):
         def step(k, carry):
             px, py, target = peer(k)
-            remote(src.at[pl.ds(pl.multiple_of(target * rows, 8), rows), :], dst_of(me), number, (comp, px, py))
+            remote(src.at[pl.ds(pl.multiple_of(target * rows, 8), sent), :], dst_of(me), number, (comp, px, py))
             return carry
 
         for k in far_first(NX, NY):
@@ -274,18 +292,8 @@
 
     mine16 = pl.ds(pl.multiple_of(me * 16, 16), 16)
     mine8 = pl.ds(pl.multiple_of(me * 8, 8), 8)
-    pl.semaphore_wait(row_here.at[0], NX - 1)
-    exchange(A1, 16, MSG, lambda m: R1.at[pl.ds(pl.multiple_of(m * 16, 16), 16), :])
+    exchange(A1, 16, 14, MSG, lambda m: R1.at[pl.ds(pl.multiple_of(m * 16, 16), 14), :])
     R1[mine16, :] = MSG[mine16, :]
-
-    loads[1].wait()
-
-    def pack_first(f, carry):
-        pack_atmos(S, rf_t, rf_b, kf, f)
-        return carry
-
-    lax.fori_loop(0, NF, pack_first, 0)
-    full_halo = halo(FULL, rf_t, rf_b, kf, hf_a, hf_b, hf_l, hf_r, dev_down, dev_up)
 
     for copy in ocean_halo:
         copy.wait_recv()
@@ -337,11 +345,32 @@
 
     lax.fori_loop(0, 16, split_o, 0)
 
-    arrived(A1, R1.at[pl.ds(0, 16 * (peers - 1)), :])
-    chosen = (R1[pl.ds(7, 128, stride=8), :] == (lane128 - jnp.where(low128, 0, 64)).astype(F32)).astype(F32)
+    loads[1].wait()
+
+    def pack_first(f, carry):
+        pack_atmos(S, rf_t, rf_b, kf, f)
+        return carry
+
+    lax.fori_loop(0, NF, pack_first, 0)
+    full_halo = halo(FULL, rf_t, rf_b, kf, hf_a, hf_b, hf_l, hf_r, dev_down, dev_up)
+
+    arrived(LABELS, NOTES.at[pl.ds(0, peers - 1)])
+    notes = NOTES[:, 0, :]
+    slots = pltpu.roll(notes, 112, 1)
+    labels = []
+    for c in range(2):
+        hit = notes == (2 * me + c).astype(F32)
+        of_e = jnp.sum(jnp.where(hit & (lane64 < 16), slots, 0.0), axis=1, keepdims=True) - 1.0
+        of_o = jnp.sum(jnp.where(hit & (lane64 >= 32) & (lane64 < 48), slots, 0.0), axis=1, keepdims=True) - 1.0
+        labels.append(jnp.where(lane64 < 64, of_o, of_e))
+    lane128 = lax.broadcasted_iota(jnp.int32, (128, 128), 1)
+    place = (lane128 - jnp.where(lane128 < 64, 0, 64)).astype(F32)
+    chosen = (jnp.concatenate(labels, axis=0) == place).astype(F32)
     QM[...] = chosen.astype(BF16)
     PT[...] = jnp.transpose(chosen).astype(BF16)
-    fields = [halves(PT[pl.ds(64, 16), :], split_cat(R1[pl.ds(f, 128, stride=8), :])) for f in range(7)]
+
+    arrived(A1, R1.at[pl.ds(0, 14 * (peers - 1)), :])
+    fields = [halves(PT[pl.ds(64, 16), :], split_cat(both_ranks(R1, f, 7, 16))) for f in range(7)]
     heat, salt, east, north, gain, fresh, shape = fields
     speed = jnp.sqrt(east * east + north * north + 0.5)
     flux = [
@@ -364,7 +393,7 @@
         return carry
 
     lax.fori_loop(0, peers // 8, pack_mapped, 0)
-    exchange(A2, 8, MSG2, lambda m: R2.at[pl.ds(pl.multiple_of(m * 8, 8), 8), :])
+    exchange(A2, 8, 8, MSG2, lambda m: R2.at[pl.ds(pl.multiple_of(m * 8, 8), 8), :])
     R2[mine8, :] = MSG2[mine8, :]
 
     for copy in full_halo:
@@ -395,7 +424,7 @@
 
     arrived(A2, R2.at[pl.ds(0, 8 * (peers - 1)), :])
     for g in range(NO):
-        FOR[pl.ds(64 * g, 64), :] = halves(PT[pl.ds(0, 64), :], split_cat(R2[pl.ds(g, 128, stride=4), :]))
+        FOR[pl.ds(64 * g, 64), :] = halves(PT[pl.ds(0, 64), :], split_cat(both_ranks(R2, g, 4, 8)))
     twin_copy = remote(FOR, FORIN, COMP, twin)
     zero64 = jnp.zeros((64, 256), BF16)
     for g in range(NO):
@@ -410,8 +439,8 @@
         ON[rows, :] = top
         TOPC[g, pl.ds(0, 64), :] = split_cat(top)
     for g in range(NO):
-        ANS[pl.ds(g, 128, stride=4), :] = halves(QM[...], TOPC[g])
-    exchange(A3, 8, ANS, lambda m: B3.at[m])
+        put_ranks(ANS, g, halves(QM[...], TOPC[g]))
+    exchange(A3, 8, 8, ANS, lambda m: B3.at[m])
     B3[me] = ANS[mine8, :]
     second_halo = halo(SECOND, r2_t, r2_b, k2, h2_a, h2_b, h2_l, h2_r, dev_down, dev_up)
     ocean_store = pltpu.make_async_copy(ON, ocean_out, out_sem.at[0])
@@ -426,8 +455,8 @@
     for g in range(NO):
         OEC[g, pl.ds(64, 16), :] = split_cat(OE[pl.ds(16 * g, 16), :])
     for g in range(NO):
-        REP[pl.ds(g, 128, stride=4), :] = halves(QM[...], OEC[g])
-    exchange(A4, 8, REP, lambda m: B4.at[m])
+        put_ranks(REP, g, halves(QM[...], OEC[g]))
+    exchange(A4, 8, 8, REP, lambda m: B4.at[m])
     B4[me] = REP[mine8, :]
 
     for copy in second_halo:
@@ -451,7 +480,8 @@
 
     for copy in surface_halo + full_halo + ocean_halo + second_halo + [twin_copy]:
         copy.wait_send()
-    departed(A1, MSG.at[pl.ds(0, 16 * (peers - 1)), :])
+    departed(A1, MSG.at[pl.ds(0, 14 * (peers - 1)), :])
+    departed(LABELS, NOTES.at[pl.ds(0, peers - 1)])
     departed(A2, MSG2.at[pl.ds(0, 8 * (peers - 1)), :])
     departed(A3, ANS.at[pl.ds(0, 8 * (peers - 1)), :])
     departed(A4, REP.at[pl.ds(0, 8 * (peers - 1)), :])
@@ -491,7 +521,7 @@
         + halo_atmos
         + halo_atmos
         + [vm(40, 128), vm(40, 128), vm(64, 128), vm(40, 128), vm(40, 128), vm(64, 128), vm(64, 128)]
-        + [vm(128, 128), vm(16, 8, 128), vm(16 * peers, 128), vm(16 * peers, 128)]
+        + [vm(1, 1, 128), vm(peers, 1, 128), vm(128, 128), vm(16, 8, 128), vm(16, 8, 128), vm(16 * peers, 128), vm(16 * peers, 128)]
         + [vm(128, 128, dtype=BF16), vm(128, 128, dtype=BF16), vm(128, 128), vm(16, 8, 128)]
         + [vm(8 * peers, 128), vm(8 * peers, 128), vm(256, 128), vm(256, 128)]
         + [vm(NO, 128, 256, dtype=BF16), vm(8 * peers, 128), vm(peers, 8, 128), vm(64, 128)]

time: 50.9 us -> 50 us (0.982)
  Pallas kernels: 50.1 us -> 49.2 us
    pallas_call x1, Pallas kernels: 48.6 us -> 47.7 us  [on_device(): pl.pallas_call(functools.partial(kernel, sizes), out_shape=(jax.ShapeDtyp...]
where the time goes in v4:
time: 50 us; the launch traced here: 49.8 us
  Pallas kernels  49.2 us (98%)
  between operations  0.64 us (1%)
    pallas_call x1, Pallas kernels, on_device(): pl.pallas_call(functools.partial(kernel, sizes), out_shape=(jax.ShapeDtyp...  47.7 us
    pallas_call x1, Pallas kernels, on_device(): pl.pallas_call(hand_out, out_shape=tuple((jax.ShapeDtypeStruct(x.shape, x...  1.54 us

profile of v4, /device:TPU:1, one launch (start us, length us, event | category | flops | bytes accessed | tf_op | source)
XLA Modules:
  0.0 49.8 jit_solution(1270465199764368465)
XLA Ops:
  0.6 47.7 %shard_map.130 = (f32[10,320,128]{2,1,0:T(8,128)S(1)}, f32[2048,128]{1,0:T(8,128)S(1)}, f32[64,128]{1,0:T(8,128)S(1)}) custom-call(f32[10,320,128]{2,1,0:T(8,128)} %bitcast.7, f32[16,128,128]{2,1,0:T(8,128)} %remap_a.1, f32[16,128,128]{2,1,0:T(8,128)} %remap_o.1, f32[2048,128]{1,0:T(8,128)} %bitcast.8, s32[64,128]{1,0:T(8,128)} %wet_in.1, f32[10]{0:T(128)} %diff_in.1, ...), custom_call_target="tpu_custom_call" | custom-call | tf_op jit(solution)/shard_map/pallas_call | solution.py:540
  48.3 1.5 %shard_map.131 = (f32[10,320,128]{2,1,0:T(8,128)}, f32[2048,128]{1,0:T(8,128)}, f32[64,128]{1,0:T(8,128)}) custom-call(f32[10,320,128]{2,1,0:T(8,128)S(1)} %get-tuple-element.9.a, f32[2048,128]{1,0:T(8,128)S(1)} %get-tuple-element.10.b, f32[64,128]{1,0:T(8,128)S(1)} %get-tuple-element.11.c), custom_call_target="tpu_custom_call" | custom-call | tf_op jit(solution)/shard_map/pallas_call | solution.py:562

commit v5 on v4

--- a/solution.py
+++ b/solution.py
@@ -22,8 +22,8 @@
         for at in range(n):
             to = (at + offset) % n
             ahead = (to - at) % 4
-            total += min(ahead, 4 - ahead) + flip * (to // 4 != at // 4)
-        return total / n
+            total = max(total, min(ahead, 4 - ahead) + flip * (to // 4 != at // 4))
+        return total
 
     return sorted(range(1, nx * ny), key=lambda k: (-way(nx, k // ny, 2) - way(ny, k % ny, 1), k))
 

time: 50 us -> 47.6 us (0.952)
  Pallas kernels: 49.2 us -> 46.9 us
    pallas_call x1, Pallas kernels: 47.7 us -> 45.3 us  [on_device(): pl.pallas_call(functools.partial(kernel, sizes), out_shape=(jax.ShapeDtyp...]
where the time goes in v5:
time: 47.6 us; the launch traced here: 47.5 us
  Pallas kernels  46.9 us (99%)
  between operations  0.64 us (1%)
    pallas_call x1, Pallas kernels, on_device(): pl.pallas_call(functools.partial(kernel, sizes), out_shape=(jax.ShapeDtyp...  45.3 us
    pallas_call x1, Pallas kernels, on_device(): pl.pallas_call(hand_out, out_shape=tuple((jax.ShapeDtypeStruct(x.shape, x...  1.54 us

profile of v5, /device:TPU:1, one launch (start us, length us, event | category | flops | bytes accessed | tf_op | source)
XLA Modules:
  0.0 47.5 jit_solution(16345934157813596671)
XLA Ops:
  0.6 45.3 %shard_map.130 = (f32[10,320,128]{2,1,0:T(8,128)S(1)}, f32[2048,128]{1,0:T(8,128)S(1)}, f32[64,128]{1,0:T(8,128)S(1)}) custom-call(f32[10,320,128]{2,1,0:T(8,128)} %bitcast.7, f32[16,128,128]{2,1,0:T(8,128)} %remap_a.1, f32[16,128,128]{2,1,0:T(8,128)} %remap_o.1, f32[2048,128]{1,0:T(8,128)} %bitcast.8, s32[64,128]{1,0:T(8,128)} %wet_in.1, f32[10]{0:T(128)} %diff_in.1, ...), custom_call_target="tpu_custom_call" | custom-call | tf_op jit(solution)/shard_map/pallas_call | solution.py:540
  46.0 1.5 %shard_map.131 = (f32[10,320,128]{2,1,0:T(8,128)}, f32[2048,128]{1,0:T(8,128)}, f32[64,128]{1,0:T(8,128)}) custom-call(f32[10,320,128]{2,1,0:T(8,128)S(1)} %get-tuple-element.9.a, f32[2048,128]{1,0:T(8,128)S(1)} %get-tuple-element.10.b, f32[64,128]{1,0:T(8,128)S(1)} %get-tuple-element.11.c), custom_call_target="tpu_custom_call" | custom-call | tf_op jit(solution)/shard_map/pallas_call | solution.py:562

commit v6 on v5

--- a/solution.py
+++ b/solution.py
@@ -25,7 +25,7 @@
             total = max(total, min(ahead, 4 - ahead) + flip * (to // 4 != at // 4))
         return total
 
-    return sorted(range(1, nx * ny), key=lambda k: (-way(nx, k // ny, 2) - way(ny, k % ny, 1), k))
+    return sorted(range(1, nx * ny), key=lambda k: (-way(nx, k // ny, 2), -way(ny, k % ny, 1), k))
 
 
 def split_cat(x):
@@ -73,7 +73,7 @@
     r2_t, r2_b, k2, h2_a, h2_b, h2_l, h2_r,
     ro_t, ro_b, ko, ho_a, ho_b, ho_l, ho_r,
     NOTE, NOTES, X, pieces, shifted, MSG, R1, QM, PT, FL, mapped, MSG2, R2, FOR, FORIN,
-    TOPC, ANS, B3, OE, OEC, REP, B4, OSV,
+    TOPC, ANS, B3, OE, OEC, REP, B4,
     diff, e_owner, e_slot, o_owner, o_slot, mixing,
     tab_v, tab_s,
     in_sem, out_sem, tab_sem, send, recv, row_here,
@@ -98,14 +98,6 @@
         py = lax.rem(gy + lax.rem(k, NY), NY)
         return px, py, px * NY + py
 
-    barrier = pltpu.get_barrier_semaphore()
-
-    row_peers = [(comp, gx, lax.rem(gy + b, NY)) for b in range(1, NY)]
-    column_peers = [(comp, lax.rem(gx + a, NX), gy) for a in range(1, NX)]
-    greeted = row_peers + column_peers + [dev_down, dev_up, twin]
-    for other in greeted:
-        pl.semaphore_signal(barrier, inc=1, device_id=other, device_id_type=MESH)
-
     top_rows = 16 * (LEV - 2)
     loads = [
         pltpu.make_async_copy(state.at[:, pl.ds(top_rows, 32), :], S.at[:, pl.ds(top_rows, 32), :], in_sem.at[0]),
@@ -122,7 +114,17 @@
             (diff_in, diff), (mixing_in, mixing),
         ])
     ]
-    for load in small + loads:
+    loads[0].start()
+
+    barrier = pltpu.get_barrier_semaphore()
+
+    row_peers = [(comp, gx, lax.rem(gy + b, NY)) for b in range(1, NY)]
+    column_peers = [(comp, lax.rem(gx + a, NX), gy) for a in range(1, NX)]
+    greeted = row_peers + column_peers + [dev_down, dev_up, twin]
+    for other in greeted:
+        pl.semaphore_signal(barrier, inc=1, device_id=other, device_id_type=MESH)
+
+    for load in small + loads[1:]:
         load.start()
 
     lane16 = lax.broadcasted_iota(jnp.int32, (16, 128), 1)
@@ -474,9 +476,7 @@
     for i in range(16):
         both = quad(split_stack(B4[e_owner[i]]), MAT[i])
         picked = jnp.where(e_rank[i] == 0, both, pltpu.roll(both, 4, 0))
-        OSV[pl.ds(i, 4, stride=16), :] = picked[0:4]
-    surf_store = pltpu.make_async_copy(OSV, surf_out, out_sem.at[2])
-    surf_store.start()
+        surf_out[pl.ds(i, 4, stride=16), :] = picked[0:4]
 
     for copy in surface_halo + full_halo + ocean_halo + second_halo + [twin_copy]:
         copy.wait_send()
@@ -487,7 +487,6 @@
     departed(A4, REP.at[pl.ds(0, 8 * (peers - 1)), :])
     ocean_store.wait()
     atmos_store.wait()
-    surf_store.wait()
 
 
 def hand_out(a, b, c, a_out, b_out, c_out, sem):
@@ -525,7 +524,7 @@
         + [vm(128, 128, dtype=BF16), vm(128, 128, dtype=BF16), vm(128, 128), vm(16, 8, 128)]
         + [vm(8 * peers, 128), vm(8 * peers, 128), vm(256, 128), vm(256, 128)]
         + [vm(NO, 128, 256, dtype=BF16), vm(8 * peers, 128), vm(peers, 8, 128), vm(64, 128)]
-        + [vm(NO, 128, 256, dtype=BF16), vm(8 * peers, 128), vm(peers, 8, 128), vm(64, 128)]
+        + [vm(NO, 128, 256, dtype=BF16), vm(8 * peers, 128), vm(peers, 8, 128)]
         + [pltpu.SMEM((NF,), F32)] + [pltpu.SMEM((16,), jnp.int32) for _ in range(4)] + [pltpu.SMEM((NO,), F32)]
         + [vm(8, 128, dtype=jnp.int32), pltpu.SMEM((8, 128), jnp.int32)]
         + [
@@ -545,7 +544,7 @@
             jax.ShapeDtypeStruct((64, 128), F32),
         ),
         in_specs=[hbm] * 11,
-        out_specs=(any_, any_, any_),
+        out_specs=(any_, any_, pl.BlockSpec(memory_space=pltpu.VMEM)),
         scratch_shapes=scratch,
         compiler_params=pltpu.CompilerParams(
             collective_id=0, has_side_effects=True, vmem_limit_bytes=40 * 1024 * 1024

time: 47.6 us -> 47.4 us (level)
  no operation moved by 1% of the time
where the time goes in v6:
time: 47.4 us; the launch traced here: 47.2 us
  Pallas kernels  46.6 us (98%)
  between operations  0.64 us (1%)
    pallas_call x1, Pallas kernels, on_device(): pl.pallas_call(functools.partial(kernel, sizes), out_shape=(jax.ShapeDtyp...  45.1 us
    pallas_call x1, Pallas kernels, on_device(): pl.pallas_call(hand_out, out_shape=tuple((jax.ShapeDtypeStruct(x.shape, x...  1.54 us

profile of v6, /device:TPU:1, one launch (start us, length us, event | category | flops | bytes accessed | tf_op | source)
XLA Modules:
  0.0 47.2 jit_solution(13079239177060165607)
XLA Ops:
  0.6 45.1 %shard_map.130 = (f32[10,320,128]{2,1,0:T(8,128)S(1)}, f32[2048,128]{1,0:T(8,128)S(1)}, f32[64,128]{1,0:T(8,128)S(1)}) custom-call(f32[10,320,128]{2,1,0:T(8,128)} %bitcast.7, f32[16,128,128]{2,1,0:T(8,128)} %remap_a.1, f32[16,128,128]{2,1,0:T(8,128)} %remap_o.1, f32[2048,128]{1,0:T(8,128)} %bitcast.8, s32[64,128]{1,0:T(8,128)} %wet_in.1, f32[10]{0:T(128)} %diff_in.1, ...), custom_call_target="tpu_custom_call" | custom-call | tf_op jit(solution)/shard_map/pallas_call | solution.py:539
  45.7 1.5 %shard_map.131 = (f32[10,320,128]{2,1,0:T(8,128)}, f32[2048,128]{1,0:T(8,128)}, f32[64,128]{1,0:T(8,128)}) custom-call(f32[10,320,128]{2,1,0:T(8,128)S(1)} %get-tuple-element.9.a, f32[2048,128]{1,0:T(8,128)S(1)} %get-tuple-element.10.b, f32[64,128]{1,0:T(8,128)S(1)} %get-tuple-element.11.c), custom_call_target="tpu_custom_call" | custom-call | tf_op jit(solution)/shard_map/pallas_call | solution.py:561
